TPU v7x, 512 devices: a whole 4x8x8 slice. The times are simulated.
512 devices in a mesh: dp: 4 (over x), expert: 16 (over z, core), etp: 8 (over y).
Axes of the slice: x: 4, y: 8, z: 8, core: 2. Of those that a mesh axis runs over, the one named last changes fastest.
Arguments:
- tokens: bfloat16 [9728, 4096], P(('dp', 'expert'), 'etp'), may hold values from -6 to 6
- cotangent: bfloat16 [9728, 4096], P(('dp', 'expert'), 'etp'), may hold values from -6 to 6
- gates: bfloat16 [9728, 8], P(('dp', 'expert')), may hold values from 0.049804688 to 0.5
- experts_hit: int32 [9728, 8], P(('dp', 'expert')), may hold values from -1 to 15, as said below
- positions: int32 [9728, 8], P(('dp', 'expert')), may hold values from -1 to 18, as said below
- gate_w: bfloat16 [16, 4096, 1536], P('expert', 'dp', 'etp'), may hold values from -0.09375 to 0.09375
- up_w: bfloat16 [16, 4096, 1536], P('expert', 'dp', 'etp'), may hold values from -0.09375 to 0.09375
- down_w: bfloat16 [16, 1536, 4096], P('expert', 'etp', 'dp'), may hold values from -0.15625 to 0.15625
Outputs:
- input_grad: bfloat16 [9728, 4096], P(('dp', 'expert'), 'etp')
- down_grad: bfloat16 [16, 1536, 4096], P('expert', 'etp', 'dp')
Inputs may be any that keep to these rules, and one draw needn't show every extreme that they name: experts_hit and positions are -1 together, for routes to experts outside these 16. In the rows of one device, the routes to one expert hold positions 0 to n - 1 once each, with n between 1 and 19; no token names an expert twice. `positions`: see experts_hit.
All inputs are finite; a program needn't handle non-finite values.
Results may differ from a plain program's by a relative error of at most 0.018.
Values may be sent and summed in bfloat16 or wider, within the bound.
No kernel may reach another device: no remote copies, remote signals or barrier semaphores. Data moves between devices by JAX's collectives and lax.ppermute only.
A program may use at most 64 MiB of HBM per device.

v0:
```python
import jax
import jax.numpy as jnp
from jax import lax
from jax.sharding import PartitionSpec as P

CAP = 19


def expert_grads(feats, grads, gate_col, w_gate, w_up, w_down):
    gate_pre = jnp.dot(feats, w_gate, preferred_element_type=jnp.float32)
    up_pre = jnp.dot(feats, w_up, preferred_element_type=jnp.float32)
    sig = jax.nn.sigmoid(gate_pre)
    act = gate_pre * sig
    hidden_b = (act * up_pre).astype(jnp.bfloat16)
    back = lax.dot_general(
        grads, w_down, (((1,), (1,)), ((), ())), preferred_element_type=jnp.float32
    )
    gate_f = gate_col.astype(jnp.float32)[:, None]
    d_hidden = gate_f * back
    d_gate_b = (d_hidden * up_pre * sig * (1.0 + gate_pre * (1.0 - sig))).astype(jnp.bfloat16)
    d_up_b = (d_hidden * act).astype(jnp.bfloat16)
    d_part = lax.dot_general(
        d_gate_b, w_gate, (((1,), (1,)), ((), ())), preferred_element_type=jnp.float32
    )
    d_part = d_part + lax.dot_general(
        d_up_b, w_up, (((1,), (1,)), ((), ())), preferred_element_type=jnp.float32
    )
    scaled = (gate_f * grads).astype(jnp.bfloat16)
    term = lax.dot_general(
        hidden_b, scaled, (((0,), (0,)), ((), ())), preferred_element_type=jnp.float32
    )
    return (d_part.astype(jnp.bfloat16), term)


def local(tokens, cotangent, gates, experts_hit, positions, gate_w, up_w, down_w):
    width = lax.axis_size("expert")
    rows_dev = tokens.shape[0]
    routes = experts_hit.shape[1]
    slots = width * CAP
    valid = experts_hit >= 0
    flat = jnp.where(valid, experts_hit * CAP + positions, slots)
    flat_all = flat.reshape(-1)
    token_ids = jnp.repeat(jnp.arange(rows_dev, dtype=jnp.int32), routes)
    owner = jnp.zeros((slots + 1,), jnp.int32).at[flat_all].set(token_ids)[:slots]
    filled = jnp.zeros((slots + 1,), jnp.bool_).at[flat_all].set(True)[:slots]
    slot_gate = jnp.zeros((slots + 1,), jnp.bfloat16).at[flat_all].set(gates.reshape(-1))[:slots]
    slot_gate = slot_gate.reshape(width, CAP)

    def pack(source):
        rows = jnp.where(filled[:, None], source[owner], jnp.zeros((), source.dtype))
        return rows.reshape(width, CAP, source.shape[1])

    full_x, full_dy = (
        lax.all_gather(tokens, "etp", axis=1, tiled=True),
        lax.all_gather(cotangent, "etp", axis=1, tiled=True),
    )
    recv_x, recv_dy, recv_gate = (
        lax.all_to_all(pack(full_x), "expert", split_axis=0, concat_axis=0, tiled=True),
        lax.all_to_all(pack(full_dy), "expert", split_axis=0, concat_axis=0, tiled=True),
        lax.all_to_all(slot_gate, "expert", split_axis=0, concat_axis=0, tiled=True),
    )
    full_width = recv_x.shape[2]
    feats = recv_x.reshape(slots, full_width)
    grads = recv_dy.reshape(slots, full_width)
    w_gate, w_up, w_down = (
        lax.all_gather(gate_w[0], "dp", axis=0, tiled=True),
        lax.all_gather(up_w[0], "dp", axis=0, tiled=True),
        lax.all_gather(down_w[0], "dp", axis=1, tiled=True),
    )
    d_part_b, term = expert_grads(feats, grads, recv_gate.reshape(slots), w_gate, w_up, w_down)
    down_grad = lax.psum_scatter(term.astype(jnp.bfloat16), "dp", scatter_dimension=1, tiled=True)[
        None
    ]
    summed = lax.psum_scatter(
        d_part_b.astype(jnp.float32).astype(jnp.bfloat16), "etp", scatter_dimension=1, tiled=True
    ).astype(jnp.float32)
    returned = lax.all_to_all(
        summed.reshape(width, CAP, summed.shape[1]).astype(jnp.bfloat16),
        "expert",
        split_axis=0,
        concat_axis=0,
        tiled=True,
    ).astype(jnp.float32)
    narrow = returned.shape[2]
    table = jnp.concatenate(
        [returned.reshape(slots, narrow), jnp.zeros((1, narrow), jnp.float32)], axis=0
    )
    total = jnp.zeros((rows_dev, narrow), jnp.float32)
    for route in range(routes):
        total = total + table[flat[:, route]]
    input_grad = total.astype(jnp.bfloat16)
    return (input_grad, down_grad)


def solution(mesh):
    placed = (
        P(("dp", "expert"), "etp"),
        P(("dp", "expert"), "etp"),
        P(("dp", "expert"), None),
        P(("dp", "expert"), None),
        P(("dp", "expert"), None),
        P("expert", "dp", "etp"),
        P("expert", "dp", "etp"),
        P("expert", "etp", "dp"),
    )
    return jax.shard_map(
        local,
        mesh=mesh,
        in_specs=placed,
        out_specs=(P(("dp", "expert"), "etp"), P("expert", "etp", "dp")),
        check_vma=False,
    )
```

profile of v0, /device:TPU:8, one launch (start us, length us, event | category | flops | bytes accessed | tf_op | source)
XLA Modules:
  0.0 373.5 jit_solution(14487152539822425806)
XLA Ops:
  11.4 12.6 %scatter_custom_fusion = bf16[305]{0:T(512)(128)(2,1)S(1)} fusion(s32[1216]{0:T(1024)S(1)} %fusion.18, bf16[1216]{0:T(1024)(128)(2,1)S(1)} %reshape.171, bf16[]{:T(256)} %constant.9.clone.1), kind=kCustom, calls=%fused_computation.64 | custom fusion | bytes 612 | tf_op jit(solution)/shard_map/scatter | solution.py:46
  24.7 10.4 %all-to-all-start = ((bf16[16,1,19]{2,1,0:T(2,128)(2,1)}), bf16[16,1,19]{2,1,0:T(2,128)(2,1)S(1)}, u32[]{:S(2)}, u32[]{:S(2)}) async-start(bf16[16,1,19]{2,1,0:T(2,128)(2,1)} %all_to_all.20), calls=%async_computation | async-start | bytes 16384 | tf_op jit(solution)/shard_map/all_to_all | solution.py:60
  35.3 11.4 %scatter_custom_fusion.1 = pred[305]{0:T(512)(128)(4,1)S(1)} fusion(s32[1216]{0:T(1024)S(1)} %fusion.18, pred[1216]{0:T(1024)(128)(4,1)S(1)} %broadcast.66, pred[]{:T(512)} %constant.14.clone.1), kind=kCustom, calls=%fused_computation.62 | custom fusion | bytes 306 | tf_op jit(solution)/shard_map/scatter | solution.py:45
  46.8 6.4 %scatter_custom_fusion.2 = s32[305]{0:T(512)S(1)} fusion(s32[1216]{0:T(1024)S(1)} %fusion.18, s32[1216]{0:T(1024)S(1)} %reshape.187, s32[]{:T(128)} %constant.10.clone.1), kind=kCustom, calls=%fused_computation.60 | custom fusion | bytes 1224 | tf_op jit(solution)/shard_map/scatter | solution.py:44
  53.2 3.7 all-gather.9.cloned.1.call-done
  56.9 9.5 %gather_fusion = bf16[304,4096]{1,0:T(8,128)(2,1)} fusion(bf16[152,4096]{1,0:T(8,128)(2,1)} %all-gather.9.cloned.1.call-done, s32[1024]{0:T(1024)S(1)} %pad_clamp_fusion.8), kind=kCustom, calls=%fused_computation | custom fusion | bytes 4981952 | tf_op jit(solution)/shard_map/gather | solution.py:50
  68.5 30.9 %all-gather.11.cloned.1.call-done = bf16[152,4096]{1,0:T(8,128)(2,1)} async-done(((bf16[152,512]{1,0:T(8,128)(2,1)}), bf16[152,4096]{1,0:T(8,128)(2,1)}) %all-gather.11.cloned.1.call-update) | async-done | bytes 1245200 | tf_op jit(solution)/shard_map/all_gather | solution.py:54
  99.4 9.5 %gather_fusion.1 = bf16[304,4096]{1,0:T(8,128)(2,1)} fusion(bf16[152,4096]{1,0:T(8,128)(2,1)} %all-gather.11.cloned.1.call-done, s32[1024]{0:T(1024)S(1)} %pad_clamp_fusion.8), kind=kCustom, calls=%fused_computation.1 | custom fusion | bytes 4981952 | tf_op jit(solution)/shard_map/gather | solution.py:50
  108.9 3.4 gather.37
  112.3 5.0 %broadcast_select_fusion.1 = (bf16[16,19,4096]{2,1,0:T(8,128)(2,1)}, bf16[16,19,4096]{2,1,0:T(8,128)(2,1)}) fusion(bf16[16,19,4096]{2,1,0:T(8,128)(2,1)S(1)} %gather.35, pred[16,19]{1,0:T(8,128)(4,1)S(1)} %broadcast_in_dim.63, bf16[16,19,4096]{2,1,0:T(8,128)(2,1)} %gather.37), kind=kLoop, calls=%fused_computation.18 | loop fusion | flops 2490368 | bytes 9961776 | tf_op jit(solution)/shard_map/jit(_where)/select_n | solution.py:50
  117.3 7.5 %all-to-all-start.1 = ((bf16[16,19,4096]{2,1,0:T(8,128)(2,1)}), bf16[16,19,4096]{2,1,0:T(8,128)(2,1)S(1)}, u32[]{:S(2)}, u32[]{:S(2)}) async-start(bf16[16,19,4096]{2,1,0:T(8,128)(2,1)} %get-tuple-element.10), calls=%async_computation.1 | async-start | bytes 6291456 | tf_op jit(solution)/shard_map/all_to_all | solution.py:59
  125.3 71.2 %all-to-all-done.1 = bf16[16,19,4096]{2,1,0:T(8,128)(2,1)S(1)} async-done(((bf16[16,19,4096]{2,1,0:T(8,128)(2,1)}), bf16[16,19,4096]{2,1,0:T(8,128)(2,1)S(1)}, u32[]{:S(2)}, u32[]{:S(2)}) %all-to-all-start.1) | async-done | bytes 2490400 | tf_op jit(solution)/shard_map/all_to_all | solution.py:59
  196.5 4.7 %all-to-all-start.2 = ((bf16[16,19,4096]{2,1,0:T(8,128)(2,1)}), bf16[16,19,4096]{2,1,0:T(8,128)(2,1)}, u32[]{:S(2)}, u32[]{:S(2)}) async-start(bf16[16,19,4096]{2,1,0:T(8,128)(2,1)} %get-tuple-element.11), calls=%async_computation.2 | async-start | bytes 6291456 | tf_op jit(solution)/shard_map/all_to_all | solution.py:58
  204.8 68.2 %all-to-all-done.2 = bf16[16,19,4096]{2,1,0:T(8,128)(2,1)} async-done(((bf16[16,19,4096]{2,1,0:T(8,128)(2,1)}), bf16[16,19,4096]{2,1,0:T(8,128)(2,1)}, u32[]{:S(2)}, u32[]{:S(2)}) %all-to-all-start.2) | async-done | bytes 2490400 | tf_op jit(solution)/shard_map/all_to_all | solution.py:58
  273.0 2.3 reshape.84
  276.8 2.6 fusion.4
  279.5 3.5 fusion.7
  283.0 2.7 fusion.11
  287.2 2.3 fusion
  289.6 2.2 convolution_convert_fusion
  291.9 39.0 %reduce-scatter.3.cloned.1.call-done = bf16[304,512]{1,0:T(8,128)(2,1)} async-done(((bf16[304,4096]{1,0:T(8,128)(2,1)}), bf16[304,512]{1,0:T(8,128)(2,1)}) %reduce-scatter.3.cloned.1.call-update) | async-done | bytes 311312 | tf_op jit(solution)/shard_map/reduce_scatter | solution.py:74
  332.7 7.5 %all-to-all-start.3 = ((bf16[16,19,512]{2,1,0:T(8,128)(2,1)}), bf16[16,19,512]{2,1,0:T(8,128)(2,1)S(1)}, u32[]{:S(2)}, u32[]{:S(2)}) async-start(bf16[16,19,512]{2,1,0:T(8,128)(2,1)} %convert_element_type.47), calls=%async_computation.4 | async-start | bytes 786432 | tf_op jit(solution)/shard_map/all_to_all | solution.py:77
  340.3 13.6 %all-to-all-done.3 = bf16[16,19,512]{2,1,0:T(8,128)(2,1)S(1)} async-done(((bf16[16,19,512]{2,1,0:T(8,128)(2,1)}), bf16[16,19,512]{2,1,0:T(8,128)(2,1)S(1)}, u32[]{:S(2)}, u32[]{:S(2)}) %all-to-all-start.3) | async-done | bytes 311328 | tf_op jit(solution)/shard_map/all_to_all | solution.py:77
  361.4 4.8 %reduce-scatter.5.cloned.1.call-done = bf16[192,1024]{1,0:T(8,128)(2,1)} async-done(((bf16[192,4096]{1,0:T(8,128)(2,1)}), bf16[192,1024]{1,0:T(8,128)(2,1)}) %reduce-scatter.5.cloned.1.call-update) | async-done | bytes 393232 | tf_op jit(solution)/shard_map/reduce_scatter | solution.py:71
  (65 shorter events, 22.9 us)
Async XLA Ops:
  8.0 48.9 %all-gather.9.cloned.1.call-start = ((), (), s32[]{:S(2)}) async-start(), calls=%async_computation.6 | async-start | bytes 1400832 | tf_op jit(solution)/shard_map/all_gather | solution.py:55
  8.7 90.7 %all-gather.11.cloned.1.call-start = ((), (), s32[]{:S(2)}) async-start(), calls=%async_computation.7 | async-start | bytes 1400832 | tf_op jit(solution)/shard_map/all_gather | solution.py:54
  24.7 92.5 %all-to-all-start = ((bf16[16,1,19]{2,1,0:T(2,128)(2,1)}), bf16[16,1,19]{2,1,0:T(2,128)(2,1)S(1)}, u32[]{:S(2)}, u32[]{:S(2)}) async-start(bf16[16,1,19]{2,1,0:T(2,128)(2,1)} %all_to_all.20), calls=%async_computation | async-start | bytes 16384 | tf_op jit(solution)/shard_map/all_to_all | solution.py:60
  117.3 79.2 %all-to-all-start.1 = ((bf16[16,19,4096]{2,1,0:T(8,128)(2,1)}), bf16[16,19,4096]{2,1,0:T(8,128)(2,1)S(1)}, u32[]{:S(2)}, u32[]{:S(2)}) async-start(bf16[16,19,4096]{2,1,0:T(8,128)(2,1)} %get-tuple-element.10), calls=%async_computation.1 | async-start | bytes 6291456 | tf_op jit(solution)/shard_map/all_to_all | solution.py:59
  124.7 150.7 %all-gather.17.cloned.1.call-start = ((), (), s32[]{:S(2)}) async-start(), calls=%async_computation.12 | async-start | bytes 1966080 | tf_op jit(solution)/shard_map/all_gather | solution.py:66
  196.5 76.5 %all-to-all-start.2 = ((bf16[16,19,4096]{2,1,0:T(8,128)(2,1)}), bf16[16,19,4096]{2,1,0:T(8,128)(2,1)}, u32[]{:S(2)}, u32[]{:S(2)}) async-start(bf16[16,19,4096]{2,1,0:T(8,128)(2,1)} %get-tuple-element.11), calls=%async_computation.2 | async-start | bytes 6291456 | tf_op jit(solution)/shard_map/all_to_all | solution.py:58
  201.2 78.3 %all-gather.15.cloned.1.call-start = ((), (), s32[]{:S(2)}) async-start(), calls=%async_computation.11 | async-start | bytes 1966080 | tf_op jit(solution)/shard_map/all_gather | solution.py:67
  201.8 81.2 %all-gather.13.cloned.1.call-start = ((), (), s32[]{:S(2)}) async-start(), calls=%async_computation.10 | async-start | bytes 1966080 | tf_op jit(solution)/shard_map/all_gather | solution.py:68
  202.4 128.5 %reduce-scatter.3.cloned.1.call-start = ((), (), s32[]{:S(2)}) async-start(), calls=%async_computation.8 | async-start | bytes 2801664 | tf_op jit(solution)/shard_map/reduce_scatter | solution.py:74
  275.4 1.5 copy-start.1
  279.4 3.6 copy-start
  283.0 2.7 copy-start.3
  285.8 1.4 copy-start.2
  289.5 76.7 %reduce-scatter.5.cloned.1.call-start = ((), (), s32[]{:S(2)}) async-start(), calls=%async_computation.9 | async-start | bytes 1966080 | tf_op jit(solution)/shard_map/reduce_scatter | solution.py:71
  332.7 21.2 %all-to-all-start.3 = ((bf16[16,19,512]{2,1,0:T(8,128)(2,1)}), bf16[16,19,512]{2,1,0:T(8,128)(2,1)S(1)}, u32[]{:S(2)}, u32[]{:S(2)}) async-start(bf16[16,19,512]{2,1,0:T(8,128)(2,1)} %convert_element_type.47), calls=%async_computation.4 | async-start | bytes 786432 | tf_op jit(solution)/shard_map/all_to_all | solution.py:77
Sparse Core Ops, SparseCore 0:
  10.9 45.9 all-gather.8
  59.0 40.4 all-gather.10
  289.7 41.1 reduce-scatter.2
  334.4 31.7 reduce-scatter.4
Sparse Core Ops, SparseCore 1:
  127.3 30.4 all-gather.16
  203.8 30.4 all-gather.14
  236.2 31.8 all-gather.12
where the time goes:
time: 374 us
  waiting for transfers between devices  234 us (63%)
  local copies, waits for them, and re-layouts  71.7 us (19%)
  starting transfers between devices  30.6 us (8%)
  between operations  15.8 us (4%)
  matrix products  14.3 us (4%)
  other arithmetic  6.76 us (2%)
    all_to_all x1, waiting for transfers between devices, local(): lax.all_to_all(pack(full_dy), 'expert', split_axis=0, concat_axis=0, tile...  71.2 us
    all_to_all x1, waiting for transfers between devices, local(): lax.all_to_all(pack(full_x), 'expert', split_axis=0, concat_axis=0, tiled...  68.2 us
    reduce_scatter x1, waiting for transfers between devices, local(): lax.psum_scatter(d_part_b.astype(jnp.float32).astype(jnp.bfloat16), 'etp'...  39 us
    all_gather x1, waiting for transfers between devices, local(): lax.all_gather(tokens, 'etp', axis=1, tiled=True)  30.9 us
    gather x4, local copies, waits for them, and re-layouts, pack(): source[owner]  24.5 us
    all_to_all x1, waiting for transfers between devices, local(): lax.all_to_all(summed.reshape(width, CAP, summed.shape[1]).astype(jnp.bfl...  13.6 us
    scatter x1, local copies, waits for them, and re-layouts, local(): jnp.zeros((slots + 1,), jnp.bfloat16).at[flat_all].set(gates.reshape(-1))  12.6 us
    scatter x1, local copies, waits for them, and re-layouts, local(): filled = jnp.zeros((slots + 1,), jnp.bool_).at[flat_all].set(True)[:slots]  11.4 us
  transfers between devices with their start and end apart: 11, of which 7 were waited for; matrix products, arithmetic and copies ran while one was open for 23% of the time, Pallas kernels for 0%

commit v1 on v0

--- a/solution.py
+++ b/solution.py
@@ -4,6 +4,14 @@
 from jax.sharding import PartitionSpec as P
 
 CAP = 19
+
+
+def gather_by_exchange(shard, axis, dim):
+    size = lax.axis_size(axis)
+    repeats = [size if d == dim else 1 for d in range(shard.ndim)]
+    return lax.all_to_all(
+        jnp.tile(shard, repeats), axis, split_axis=dim, concat_axis=dim, tiled=True
+    )
 
 
 def expert_grads(feats, grads, gate_col, w_gate, w_up, w_down):
@@ -51,7 +59,7 @@
         return rows.reshape(width, CAP, source.shape[1])
 
     full_x, full_dy = (
-        lax.all_gather(tokens, "etp", axis=1, tiled=True),
+        gather_by_exchange(tokens, "etp", 1),
         lax.all_gather(cotangent, "etp", axis=1, tiled=True),
     )
     recv_x, recv_dy, recv_gate = (

time: 374 us -> 346 us (0.925)
  waiting for transfers between devices: 234 us -> 201 us
  starting transfers between devices: 30.6 us -> 40.5 us
  local copies, waits for them, and re-layouts: 71.7 us -> 67.6 us
    all_gather x1 -> x0, waiting for transfers between devices: 30.9 us -> none  [local(): lax.all_gather(tokens, 'etp', axis=1, tiled=True)]
    all_to_all x0 -> x1, starting transfers between devices: none -> 9.29 us  [gather_by_exchange(): lax.all_to_all(jnp.tile(shard, repeats), axis, split_axis=dim, concat_axi...]
    gather x4, local copies, waits for them, and re-layouts: 24.5 us -> 18.8 us  [pack(): source[owner]]
  transfers between devices with their start and end apart: 11 -> 11, of which waited for: 7 -> 6; matrix products, arithmetic and copies ran while one was open for 23% -> 22% of each run, Pallas kernels for 0% -> 0%
where the time goes in v1:
time: 346 us; the launch traced here: 345 us
  waiting for transfers between devices  201 us (58%)
  local copies, waits for them, and re-layouts  67.6 us (20%)
  starting transfers between devices  40.5 us (12%)
  between operations  15.9 us (5%)
  matrix products  14.3 us (4%)
  other arithmetic  6.03 us (2%)
    all_to_all x1, waiting for transfers between devices, local(): lax.all_to_all(pack(full_dy), 'expert', split_axis=0, concat_axis=0, tile...  71.2 us
    all_to_all x1, waiting for transfers between devices, local(): lax.all_to_all(pack(full_x), 'expert', split_axis=0, concat_axis=0, tiled...  68.2 us
    reduce_scatter x1, waiting for transfers between devices, local(): lax.psum_scatter(d_part_b.astype(jnp.float32).astype(jnp.bfloat16), 'etp'...  40.7 us
    gather x4, local copies, waits for them, and re-layouts, pack(): source[owner]  18.8 us
    all_to_all x1, waiting for transfers between devices, local(): lax.all_to_all(summed.reshape(width, CAP, summed.shape[1]).astype(jnp.bfl...  13.6 us
    scatter x1, local copies, waits for them, and re-layouts, local(): jnp.zeros((slots + 1,), jnp.bfloat16).at[flat_all].set(gates.reshape(-1))  12.8 us
    all_to_all x1, starting transfers between devices, local(): lax.all_to_all(slot_gate, 'expert', split_axis=0, concat_axis=0, tiled=True)  11.5 us
    scatter x1, local copies, waits for them, and re-layouts, local(): filled = jnp.zeros((slots + 1,), jnp.bool_).at[flat_all].set(True)[:slots]  11.2 us
  transfers between devices with their start and end apart: 11, of which 6 were waited for; matrix products, arithmetic and copies ran while one was open for 22% of the time, Pallas kernels for 0%

profile of v1, /device:TPU:8, one launch (start us, length us, event | category | flops | bytes accessed | tf_op | source)
XLA Modules:
  0.0 345.5 jit_solution(9665939813137873433)
XLA Ops:
  10.1 9.3 %all-to-all-start.2 = ((bf16[152,8,512]{2,0,1:T(8,128)(2,1)}), bf16[152,8,512]{2,0,1:T(8,128)(2,1)S(1)}, u32[]{:S(2)}, u32[]{:S(2)}) async-start(bf16[152,8,512]{2,0,1:T(8,128)(2,1)} %tile.2), calls=%async_computation.2 | async-start | bytes 2490368 | tf_op jit(solution)/shard_map/all_to_all | solution.py:12
  20.5 11.2 %scatter_custom_fusion.1 = pred[305]{0:T(512)(128)(4,1)S(1)} fusion(s32[1216]{0:T(1024)S(1)} %fusion.18, pred[1216]{0:T(1024)(128)(4,1)S(1)} %broadcast.69, pred[]{:T(512)} %constant.14.clone.1), kind=kCustom, calls=%fused_computation.62 | custom fusion | bytes 306 | tf_op jit(solution)/shard_map/scatter | solution.py:53
  32.1 12.8 %scatter_custom_fusion = bf16[305]{0:T(512)(128)(2,1)S(1)} fusion(s32[1216]{0:T(1024)S(1)} %fusion.18, bf16[1216]{0:T(1024)(128)(2,1)S(1)} %reshape.178, bf16[]{:T(256)} %constant.9.clone.1), kind=kCustom, calls=%fused_computation.64 | custom fusion | bytes 612 | tf_op jit(solution)/shard_map/scatter | solution.py:54
  45.6 6.4 %scatter_custom_fusion.2 = s32[305]{0:T(512)S(1)} fusion(s32[1216]{0:T(1024)S(1)} %fusion.18, s32[1216]{0:T(1024)S(1)} %reshape.194, s32[]{:T(128)} %constant.10.clone.1), kind=kCustom, calls=%fused_computation.60 | custom fusion | bytes 1224 | tf_op jit(solution)/shard_map/scatter | solution.py:52
  52.8 11.5 %all-to-all-start = ((bf16[16,1,19]{2,1,0:T(2,128)(2,1)}), bf16[16,1,19]{2,1,0:T(2,128)(2,1)S(1)}, u32[]{:S(2)}, u32[]{:S(2)}) async-start(bf16[16,1,19]{2,1,0:T(2,128)(2,1)} %all_to_all.28), calls=%async_computation | async-start | bytes 16384 | tf_op jit(solution)/shard_map/all_to_all | solution.py:68
  64.5 3.8 %gather_fusion.1 = bf16[304,4096]{1,0:T(8,128)(2,1)} fusion(bf16[152,4096]{1,0:T(8,128)(2,1)S(1)} %bitcast.31, s32[1024]{0:T(1024)S(1)} %pad_clamp_fusion.8), kind=kCustom, calls=%fused_computation.1 | custom fusion | bytes 4981952 | tf_op jit(solution)/shard_map/gather | solution.py:58
  68.3 2.2 gather.37
  70.5 9.5 %gather_fusion = bf16[304,4096]{1,0:T(8,128)(2,1)} fusion(bf16[152,4096]{1,0:T(8,128)(2,1)} %all-gather.8.cloned.1.call-done, s32[1024]{0:T(1024)S(1)} %pad_clamp_fusion.8), kind=kCustom, calls=%fused_computation | custom fusion | bytes 4981952 | tf_op jit(solution)/shard_map/gather | solution.py:58
  79.9 3.4 gather.35
  83.3 5.0 %broadcast_select_fusion.1 = (bf16[16,19,4096]{2,1,0:T(8,128)(2,1)}, bf16[16,19,4096]{2,1,0:T(8,128)(2,1)}) fusion(bf16[16,19,4096]{2,1,0:T(8,128)(2,1)} %gather.35, pred[16,19]{1,0:T(8,128)(4,1)S(1)} %broadcast_in_dim.63, bf16[16,19,4096]{2,1,0:T(8,128)(2,1)S(1)} %gather.37), kind=kLoop, calls=%fused_computation.18 | loop fusion | flops 2490368 | bytes 9961776 | tf_op jit(solution)/shard_map/jit(_where)/select_n | solution.py:58
  88.3 7.3 %all-to-all-start.1 = ((bf16[16,19,4096]{2,1,0:T(8,128)(2,1)}), bf16[16,19,4096]{2,1,0:T(8,128)(2,1)S(1)}, u32[]{:S(2)}, u32[]{:S(2)}) async-start(bf16[16,19,4096]{2,1,0:T(8,128)(2,1)} %get-tuple-element.10), calls=%async_computation.1 | async-start | bytes 6291456 | tf_op jit(solution)/shard_map/all_to_all | solution.py:67
  96.2 71.2 %all-to-all-done.1 = bf16[16,19,4096]{2,1,0:T(8,128)(2,1)S(1)} async-done(((bf16[16,19,4096]{2,1,0:T(8,128)(2,1)}), bf16[16,19,4096]{2,1,0:T(8,128)(2,1)S(1)}, u32[]{:S(2)}, u32[]{:S(2)}) %all-to-all-start.1) | async-done | bytes 2490400 | tf_op jit(solution)/shard_map/all_to_all | solution.py:67
  167.4 4.7 %all-to-all-start.3 = ((bf16[16,19,4096]{2,1,0:T(8,128)(2,1)}), bf16[16,19,4096]{2,1,0:T(8,128)(2,1)}, u32[]{:S(2)}, u32[]{:S(2)}) async-start(bf16[16,19,4096]{2,1,0:T(8,128)(2,1)} %get-tuple-element.11), calls=%async_computation.3 | async-start | bytes 6291456 | tf_op jit(solution)/shard_map/all_to_all | solution.py:66
  175.7 68.2 %all-to-all-done.3 = bf16[16,19,4096]{2,1,0:T(8,128)(2,1)} async-done(((bf16[16,19,4096]{2,1,0:T(8,128)(2,1)}), bf16[16,19,4096]{2,1,0:T(8,128)(2,1)}, u32[]{:S(2)}, u32[]{:S(2)}) %all-to-all-start.3) | async-done | bytes 2490400 | tf_op jit(solution)/shard_map/all_to_all | solution.py:66
  243.9 2.3 reshape.91
  247.7 2.6 fusion.4
  250.4 3.5 %fusion.7 = f32[304,192]{0,1:T(8,128)S(1)} fusion(bf16[304,4096]{1,0:T(8,128)(2,1)} %copy-done.1, bf16[1,4096,192]{1,2,0:T(8,128)(2,1)} %all-gather.12.cloned.1.call-done), kind=kOutput, calls=%fused_computation.25 | convolution fusion | flops 478150656 | bytes 4296704 | tf_op jit(solution)/shard_map/dot_general | solution.py:19
  253.9 2.7 fusion.11
  258.0 2.4 fusion
  260.5 2.3 convolution_convert_fusion
  262.8 40.7 %reduce-scatter.3.cloned.1.call-done = bf16[304,512]{1,0:T(8,128)(2,1)} async-done(((bf16[304,4096]{1,0:T(8,128)(2,1)}), bf16[304,512]{1,0:T(8,128)(2,1)}) %reduce-scatter.3.cloned.1.call-update) | async-done | bytes 311312 | tf_op jit(solution)/shard_map/reduce_scatter | solution.py:82
  305.3 7.3 %all-to-all-start.4 = ((bf16[16,19,512]{2,1,0:T(8,128)(2,1)}), bf16[16,19,512]{2,1,0:T(8,128)(2,1)S(1)}, u32[]{:S(2)}, u32[]{:S(2)}) async-start(bf16[16,19,512]{2,1,0:T(8,128)(2,1)} %convert_element_type.47), calls=%async_computation.5 | async-start | bytes 786432 | tf_op jit(solution)/shard_map/all_to_all | solution.py:85
  312.7 13.6 %all-to-all-done.4 = bf16[16,19,512]{2,1,0:T(8,128)(2,1)S(1)} async-done(((bf16[16,19,512]{2,1,0:T(8,128)(2,1)}), bf16[16,19,512]{2,1,0:T(8,128)(2,1)S(1)}, u32[]{:S(2)}, u32[]{:S(2)}) %all-to-all-start.4) | async-done | bytes 311328 | tf_op jit(solution)/shard_map/all_to_all | solution.py:85
  333.8 4.3 %reduce-scatter.5.cloned.1.call-done = bf16[192,1024]{1,0:T(8,128)(2,1)} async-done(((bf16[192,4096]{1,0:T(8,128)(2,1)}), bf16[192,1024]{1,0:T(8,128)(2,1)}) %reduce-scatter.5.cloned.1.call-update) | async-done | bytes 393232 | tf_op jit(solution)/shard_map/reduce_scatter | solution.py:79
  (72 shorter events, 21.6 us)
Async XLA Ops:
  8.0 12.1 %copy-start.5 = (s32[152,8]{0,1:T(8,128)S(1)}, s32[152,8]{0,1:T(8,128)}, u32[]{:S(2)}) copy-start(s32[152,8]{0,1:T(8,128)} %param.11) | copy-start | bytes 14596
  8.0 12.1 %copy-start.4 = (s32[152,8]{0,1:T(8,128)S(1)}, s32[152,8]{0,1:T(8,128)}, u32[]{:S(2)}) copy-start(s32[152,8]{0,1:T(8,128)} %param.12) | copy-start | bytes 14596
  8.0 23.8 %copy-start.6 = (bf16[152,8]{0,1:T(8,128)(2,1)S(1)}, bf16[152,8]{0,1:T(8,128)(2,1)}, u32[]{:S(2)}) copy-start(bf16[152,8]{0,1:T(8,128)(2,1)} %param.10) | copy-start | bytes 7300
  10.1 42.8 %all-to-all-start.2 = ((bf16[152,8,512]{2,0,1:T(8,128)(2,1)}), bf16[152,8,512]{2,0,1:T(8,128)(2,1)S(1)}, u32[]{:S(2)}, u32[]{:S(2)}) async-start(bf16[152,8,512]{2,0,1:T(8,128)(2,1)} %tile.2), calls=%async_computation.2 | async-start | bytes 2490368 | tf_op jit(solution)/shard_map/all_to_all | solution.py:12
  19.4 51.1 %all-gather.8.cloned.1.call-start = ((), (), s32[]{:S(2)}) async-start(), calls=%async_computation.7 | async-start | bytes 1400832 | tf_op jit(solution)/shard_map/all_gather | solution.py:63
  52.8 35.4 %all-to-all-start = ((bf16[16,1,19]{2,1,0:T(2,128)(2,1)}), bf16[16,1,19]{2,1,0:T(2,128)(2,1)S(1)}, u32[]{:S(2)}, u32[]{:S(2)}) async-start(bf16[16,1,19]{2,1,0:T(2,128)(2,1)} %all_to_all.28), calls=%async_computation | async-start | bytes 16384 | tf_op jit(solution)/shard_map/all_to_all | solution.py:68
  88.3 79.1 %all-to-all-start.1 = ((bf16[16,19,4096]{2,1,0:T(8,128)(2,1)}), bf16[16,19,4096]{2,1,0:T(8,128)(2,1)S(1)}, u32[]{:S(2)}, u32[]{:S(2)}) async-start(bf16[16,19,4096]{2,1,0:T(8,128)(2,1)} %get-tuple-element.10), calls=%async_computation.1 | async-start | bytes 6291456 | tf_op jit(solution)/shard_map/all_to_all | solution.py:67
  95.6 150.7 %all-gather.14.cloned.1.call-start = ((), (), s32[]{:S(2)}) async-start(), calls=%async_computation.12 | async-start | bytes 1966080 | tf_op jit(solution)/shard_map/all_gather | solution.py:74
  167.4 76.5 %all-to-all-start.3 = ((bf16[16,19,4096]{2,1,0:T(8,128)(2,1)}), bf16[16,19,4096]{2,1,0:T(8,128)(2,1)}, u32[]{:S(2)}, u32[]{:S(2)}) async-start(bf16[16,19,4096]{2,1,0:T(8,128)(2,1)} %get-tuple-element.11), calls=%async_computation.3 | async-start | bytes 6291456 | tf_op jit(solution)/shard_map/all_to_all | solution.py:66
  172.1 78.3 %all-gather.12.cloned.1.call-start = ((), (), s32[]{:S(2)}) async-start(), calls=%async_computation.11 | async-start | bytes 1966080 | tf_op jit(solution)/shard_map/all_gather | solution.py:75
  172.7 81.2 %all-gather.10.cloned.1.call-start = ((), (), s32[]{:S(2)}) async-start(), calls=%async_computation.10 | async-start | bytes 1966080 | tf_op jit(solution)/shard_map/all_gather | solution.py:76
  173.3 130.2 %reduce-scatter.3.cloned.1.call-start = ((), (), s32[]{:S(2)}) async-start(), calls=%async_computation.8 | async-start | bytes 2801664 | tf_op jit(solution)/shard_map/reduce_scatter | solution.py:82
  246.2 1.5 copy-start.1
  250.3 3.6 %copy-start = (bf16[304,4096]{1,0:T(8,128)(2,1)S(1)}, bf16[304,4096]{1,0:T(8,128)(2,1)}, u32[]{:S(2)}) copy-start(bf16[304,4096]{1,0:T(8,128)(2,1)} %reshape.90) | copy-start | bytes 7471108
  253.9 2.7 copy-start.3
  256.6 1.4 copy-start.2
  260.4 77.7 %reduce-scatter.5.cloned.1.call-start = ((), (), s32[]{:S(2)}) async-start(), calls=%async_computation.9 | async-start | bytes 1966080 | tf_op jit(solution)/shard_map/reduce_scatter | solution.py:79
  305.3 21.0 %all-to-all-start.4 = ((bf16[16,19,512]{2,1,0:T(8,128)(2,1)}), bf16[16,19,512]{2,1,0:T(8,128)(2,1)S(1)}, u32[]{:S(2)}, u32[]{:S(2)}) async-start(bf16[16,19,512]{2,1,0:T(8,128)(2,1)} %convert_element_type.47), calls=%async_computation.5 | async-start | bytes 786432 | tf_op jit(solution)/shard_map/all_to_all | solution.py:85
Sparse Core Ops, SparseCore 0:
  22.3 45.9 all-gather.7
  260.5 42.8 reduce-scatter.2
  307.2 30.9 reduce-scatter.4
Sparse Core Ops, SparseCore 1:
  98.2 31.4 all-gather.13
  174.7 31.3 all-gather.11
  208.0 31.8 all-gather.9
